TPU v7x, 32 devices: a whole 2x2x4 slice. The times are simulated.
32 devices in a mesh: past: 2 (over y), second: 16 (over z, x, core).
Axes of the slice: x: 2, y: 2, z: 4, core: 2. Of those that a mesh axis runs over, the one named last changes fastest.
Arguments:
- green_row: float32 [256, 64, 128], P('second'), may hold values from -4 to 4
- green_hist: float32 [8, 256, 64, 128], P('past', 'second'), may hold values from -5.25 to 5.25, as said below
- hamiltonian: float32 [64, 128], replicated, may hold values from -0.75 to 0.75
- quad_table: float32 [8], replicated, may hold values from 0.2 to 2
- weight_index: int32 [8], P('past'), may hold values from 0 to 7
- block_start: int32 [1], replicated, may hold values from 0 to 248
Outputs:
- green_next: float32 [256, 64, 128], P('second')
- change_norm: float32 [1], replicated
Inputs may be any that keep to these rules, and one draw needn't show every extreme that they name: `green_hist`: real numbers of order one; magnitudes differ between second times.
All inputs are finite; a program needn't handle non-finite values.
Results may differ from a plain program's by a relative error of at most 0.0003.
Values sent between devices are 32-bit elements; how exact they have to be, the bound alone decides.
No kernel may reach another device: no remote copies, remote signals or barrier semaphores. Data moves between devices by JAX's collectives and lax.ppermute only.
A program may use at most 64 MiB of HBM per device.

v0:
```python
import math
import jax
import jax.numpy as jnp
from jax import lax
from jax.sharding import PartitionSpec as P

coupling = 0.5
step_size = 0.25


def rotate(tiles, orbits):
    return jnp.concatenate([-tiles[..., orbits:], tiles[..., :orbits]], axis=-1)


def self_energy(tiles, orbits):
    magnitude = tiles[..., :orbits] ** 2 + tiles[..., orbits:] ** 2
    return -coupling * jnp.concatenate([magnitude, magnitude], axis=-1) * tiles


def local(green_row, green_hist, hamiltonian, quad_table, weight_index, block_start):
    orbits = hamiltonian.shape[0]
    sec_rows = green_row.shape[0]
    past_rows = green_hist.shape[0]
    total_past = past_rows * lax.axis_size("past")
    window_start = block_start[0]
    offset = lax.axis_index("second") * sec_rows
    past_first = lax.axis_index("past") * past_rows
    weights = jnp.take(quad_table, weight_index, axis=0)
    norm_scale = 1.0 / math.sqrt(orbits * total_past)
    ham_real = hamiltonian[:, :orbits]
    ham_imag = hamiltonian[:, orbits:]
    herm_real = 0.5 * (ham_real + ham_real.T)
    herm_imag = 0.5 * (ham_imag - ham_imag.T)
    right_side = jnp.stack([green_hist, self_energy(green_hist, orbits)])

    def select(tiles_in, wanted):
        local_pos = wanted - offset
        inside = (local_pos >= 0) & (local_pos < sec_rows)
        picked = jnp.take(tiles_in, jnp.clip(local_pos, 0, sec_rows - 1), axis=0)
        return jnp.where(inside[:, None, None], picked, jnp.zeros_like(picked))

    def window_of(tiles_in):
        wanted = window_start + jnp.arange(total_past, dtype=jnp.int32)
        every_tile = lax.psum(select(tiles_in, wanted), "second")
        return lax.dynamic_slice_in_dim(every_tile, past_first, past_rows, 0)

    def memory(tiles_in):
        window = window_of(tiles_in)
        weight_col = weights[:, None, None]
        left_side = jnp.stack([weight_col * self_energy(window, orbits), weight_col * window])
        left_side = jnp.stack([left_side[..., :orbits], left_side[..., orbits:]])
        contracted = jnp.einsum(
            "cqpij,qpsjk->csik", left_side, right_side, precision=lax.Precision.HIGHEST
        )
        return norm_scale * (contracted[0] + rotate(contracted[1], orbits))

    def derive(tiles_in, integral):
        first = jnp.einsum("ij,sjk->sik", herm_real, tiles_in, precision=lax.Precision.HIGHEST)
        second = jnp.einsum(
            "ij,sjk->sik", herm_imag, rotate(tiles_in, orbits), precision=lax.Precision.HIGHEST
        )
        combined = first + second + integral
        return jnp.concatenate([combined[..., orbits:], -combined[..., :orbits]], axis=-1)

    share_rows = sec_rows // lax.axis_size("past")
    share_first = lax.axis_index("past") * share_rows
    row_share = lax.dynamic_slice_in_dim(green_row, share_first, share_rows, 0)

    def shared(tiles_in):
        return lax.psum_scatter(memory(tiles_in), "past", scatter_dimension=0, tiled=True)

    def spread(piece):
        return lax.all_gather(piece, "past", axis=0, tiled=True)

    slope_one = derive(row_share, shared(green_row))
    predicted = row_share + step_size * slope_one
    predicted_full = spread(predicted)
    slope_two = derive(predicted, shared(predicted_full))
    corrected = row_share + 0.5 * step_size * (slope_one + slope_two)
    square_sum = lax.psum(jnp.sum((corrected - predicted) ** 2), ("past", "second"))
    green_next = spread(corrected)
    entry_count = sec_rows * lax.axis_size("second") * orbits * 2 * orbits
    change = jnp.sqrt(square_sum / entry_count) / step_size
    return (green_next, change.reshape(1))


def solution(mesh):
    placed = (P("second", None, None), P("past", "second", None, None), P(), P(), P("past"), P())
    return jax.shard_map(
        local, mesh=mesh, in_specs=placed, out_specs=(P("second", None, None), P()), check_vma=False
    )
```

profile of v0, /device:TPU:0, one launch (start us, length us, event | category | flops | bytes accessed | tf_op | source)
XLA Modules:
  0.0 314.5 jit_solution(17041485729284683921)
XLA Ops:
  7.2 0.0 all-reduce.3.cloned.1.call-start
  7.9 1.6 gather_fusion.1
  9.5 0.8 select_select_fusion.1
  10.3 0.0 all-reduce.3.cloned.1.call-update
  10.3 0.0 reduce-scatter.3.cloned.1.call-start
  10.4 0.7 compare_select_fusion.1
  11.1 3.0 fusion.2
  14.1 2.2 copy_bitcast_fusion
  16.2 0.6 gather_fusion
  16.9 87.6 %all-reduce.3.cloned.1.call-done = f32[8,64,128]{2,1,0:T(8,128)} async-done(((f32[8,64,128]{2,1,0:T(8,128)}), f32[8,64,128]{2,1,0:T(8,128)}) %all-reduce.3.cloned.1.call-update) | async-done | bytes 262160 | tf_op jit(solution)/shard_map/psum | solution.py:44
  104.5 1.1 fusion.31
  105.6 1.0 fusion.34
  106.6 0.1 maximum_bitcast_fusion.11
  106.8 4.1 %fusion.5 = f32[2,16,64,128]{3,2,1,0:T(8,128)S(1)} fusion(f32[1,4,16,64,128]{4,3,0,1,2:T(8,128)} %get-tuple-element.8, f32[1,4,16,64,128]{4,3,0,1,2:T(8,128)S(1)} %get-tuple-element.7, f32[1,2,4,64,64]{4,3,1,2,0:T(8,128)S(1)} %get-tuple-element.28, f32[1,2,4,64,64]{4,3,1,2,0:T(8,128)S(1)} %get-tuple-element.27), kind=kOutput, calls=%fused_computation.12 | convolution fusion | flops 1611726848 | bytes 5505024 | tf_op jit(solution)/shard_map/cqpij,qpsjk->csik/dot_general | solution.py:52
  111.0 0.2 slice_negate_fusion.1
  111.2 1.0 fusion.14
  112.2 0.0 reduce-scatter.3.cloned.1.call-update
  112.2 0.0 all-reduce.5.cloned.1.call-start
  112.3 0.1 fusion.65
  112.4 0.1 copy.49
  112.4 0.1 copy.32
  112.5 0.1 dynamic-slice_negate_fusion
  112.7 0.4 fusion.28
  113.1 14.4 %reduce-scatter.3.cloned.1.call-done = f32[8,64,128]{2,1,0:T(8,128)} async-done(((f32[16,64,128]{2,1,0:T(8,128)}), f32[8,64,128]{2,1,0:T(8,128)}) %reduce-scatter.3.cloned.1.call-update) | async-done | bytes 262160 | tf_op jit(solution)/shard_map/reduce_scatter | solution.py:70
  127.5 1.5 fusion.10
  128.9 0.1 fusion.64
  129.1 0.1 multiply_add_fusion
  129.2 8.6 %all_gather.6 = f32[16,64,128]{2,1,0:T(8,128)} all-gather(f32[8,64,128]{2,1,0:T(8,128)S(1)} %multiply_add_fusion), channel_id=1, replica_groups=mesh['past'=2,'second'=16] {'past'}, dimensions={0}, use_global_device_ids=true | all-gather | bytes 786432 | tf_op jit(solution)/shard_map/all_gather | solution.py:73
  137.9 2.3 gather_fusion.2
  140.2 1.7 select_select_fusion
  141.9 0.0 all-reduce.5.cloned.1.call-update
  142.0 0.0 reduce-scatter.5.cloned.1.call-start
  142.0 89.9 %all-reduce.5.cloned.1.call-done = f32[8,64,128]{2,1,0:T(8,128)} async-done(((f32[8,64,128]{2,1,0:T(8,128)}), f32[8,64,128]{2,1,0:T(8,128)}) %all-reduce.5.cloned.1.call-update) | async-done | bytes 262160 | tf_op jit(solution)/shard_map/psum | solution.py:44
  231.9 1.1 fusion.30
  233.0 1.0 fusion.37
  234.1 0.1 maximum_bitcast_fusion.10
  234.2 4.1 %fusion.6 = f32[2,16,64,128]{3,2,1,0:T(8,128)S(1)} fusion(f32[1,4,16,64,128]{4,3,0,1,2:T(8,128)} %get-tuple-element.8, f32[1,4,16,64,128]{4,3,0,1,2:T(8,128)S(1)} %get-tuple-element.7, f32[1,2,4,64,64]{4,3,2,1,0:T(8,128)S(1)} %get-tuple-element.24, f32[1,2,4,64,64]{4,3,2,1,0:T(8,128)S(1)} %get-tuple-element.23), kind=kOutput, calls=%fused_computation.13 | convolution fusion | flops 1611726848 | bytes 5505024 | tf_op jit(solution)/shard_map/cqpij,qpsjk->csik/dot_general | solution.py:52
  238.4 0.2 slice_negate_fusion
  238.6 1.0 fusion.12
  239.6 0.4 fusion.41
  240.0 0.1 slice_negate_fusion.3
  240.1 14.8 %reduce-scatter.5.cloned.1.call-done = f32[8,64,128]{2,1,0:T(8,128)} async-done(((f32[16,64,128]{2,1,0:T(8,128)}), f32[8,64,128]{2,1,0:T(8,128)}) %reduce-scatter.5.cloned.1.call-update) | async-done | bytes 262160 | tf_op jit(solution)/shard_map/reduce_scatter | solution.py:70
  254.9 1.4 fusion.8
  256.4 0.1 fusion.63
  256.5 0.8 multiply_reduce_fusion
  257.3 8.5 %all_gather.7 = f32[16,64,128]{2,1,0:T(8,128)S(1)} all-gather(f32[8,64,128]{2,1,0:T(8,128)S(1)} %get-tuple-element.4), channel_id=1, replica_groups=mesh['past'=2,'second'=16] {'past'}, dimensions={0}, use_global_device_ids=true | all-gather | bytes 786432 | tf_op jit(solution)/shard_map/all_gather | solution.py:73
  265.8 39.5 %psum.23 = f32[]{:T(128)} all-reduce(f32[]{:T(128)} %get-tuple-element.3), channel_id=1, replica_groups=mesh['past'=2,'second'=16] {'past','second'}, use_global_device_ids=true, to_apply=%region_5.7 | all-reduce | flops 1 | bytes 8 | tf_op jit(solution)/shard_map/psum | solution.py:80
  306.0 0.8 copy.60
  (17 shorter events, 0.2 us)
Async XLA Ops:
  7.2 9.1 %copy-start = (f32[8]{0:T(128)S(1)}, f32[8]{0:T(128)}, u32[]{:S(2)}) copy-start(f32[8]{0:T(128)} %param.11) | copy-start | bytes 100
  7.2 97.3 %all-reduce.3.cloned.1.call-start = ((), (), s32[]{:S(2)}) async-start(), calls=%async_computation.2 | async-start | bytes 524288 | tf_op jit(solution)/shard_map/psum | solution.py:44
  10.3 117.1 %reduce-scatter.3.cloned.1.call-start = ((), (), s32[]{:S(2)}) async-start(), calls=%async_computation.3 | async-start | bytes 786432 | tf_op jit(solution)/shard_map/reduce_scatter | solution.py:70
  11.1 3.0 copy-start.1
  14.1 2.8 copy-start.4
  110.9 1.3 copy-start.3
  111.0 1.6 copy-start.2
  112.2 119.7 %all-reduce.5.cloned.1.call-start = ((), (), s32[]{:S(2)}) async-start(), calls=%async_computation.4 | async-start | bytes 524288 | tf_op jit(solution)/shard_map/psum | solution.py:44
  142.0 112.9 %reduce-scatter.5.cloned.1.call-start = ((), (), s32[]{:S(2)}) async-start(), calls=%async_computation.5 | async-start | bytes 786432 | tf_op jit(solution)/shard_map/reduce_scatter | solution.py:70
Sparse Core Ops, SparseCore 0:
  12.0 92.5 all-reduce.2
  112.3 15.1 reduce-scatter.2
  142.1 89.8 all-reduce.4
  239.8 15.1 reduce-scatter.4
where the time goes:
time: 315 us; the launch traced here: 314 us
  waiting for transfers between devices  207 us (66%)
  blocking collectives  56.7 us (18%)
  other arithmetic  16.8 us (5%)
  between operations  16.5 us (5%)
  matrix products  11.9 us (4%)
  local copies, waits for them, and re-layouts  5.69 us (2%)
    psum x2, waiting for transfers between devices, window_of(): every_tile = lax.psum(select(tiles_in, wanted), 'second')  178 us
    psum x1, blocking collectives, local(): lax.psum(jnp.sum((corrected - predicted) ** 2), ('past', 'second'))  39.5 us
    reduce_scatter x2, waiting for transfers between devices, shared(): lax.psum_scatter(memory(tiles_in), 'past', scatter_dimension=0, tiled=True)  29.2 us
    all_gather x2, blocking collectives, spread(): return lax.all_gather(piece, 'past', axis=0, tiled=True)  17.2 us
    dot_general x2, matrix products, memory(): jnp.einsum('cqpij,qpsjk->csik', left_side, right_side, precision=lax.Prec...  8.27 us
  transfers between devices with their start and end apart: 4, of which 4 were waited for; matrix products, arithmetic and copies ran while one was open for 2% of the time, Pallas kernels for 0%

commit v1 on v0

--- a/solution.py
+++ b/solution.py
@@ -41,7 +41,7 @@
 
     def window_of(tiles_in):
         wanted = window_start + jnp.arange(total_past, dtype=jnp.int32)
-        every_tile = lax.psum(select(tiles_in, wanted), "second")
+        every_tile = jnp.sum(lax.all_gather(select(tiles_in, wanted), "second"), axis=0)
         return lax.dynamic_slice_in_dim(every_tile, past_first, past_rows, 0)
 
     def memory(tiles_in):

time: 315 us -> 235 us (0.75)
  waiting for transfers between devices: 207 us -> 122 us
  other arithmetic: 16.8 us -> 21.2 us
    psum x2 -> x0, waiting for transfers between devices: 178 us -> none  [window_of(): every_tile = lax.psum(select(tiles_in, wanted), 'second')]
    all_gather x0 -> x2, waiting for transfers between devices: none -> 96.8 us  [window_of(): lax.all_gather(select(tiles_in, wanted), 'second')]
    reduce_sum x0 -> x2, other arithmetic: none -> 5.67 us  [window_of(): jnp.sum(lax.all_gather(select(tiles_in, wanted), 'second'), axis=0)]
    reduce_scatter x2, waiting for transfers between devices: 29.2 us -> 25.3 us  [shared(): lax.psum_scatter(memory(tiles_in), 'past', scatter_dimension=0, tiled=True)]
  transfers between devices with their start and end apart: 4 -> 4, of which waited for: 4 -> 4; matrix products, arithmetic and copies ran while one was open for 2% -> 4% of each run, Pallas kernels for 0% -> 0%
where the time goes in v1:
time: 235 us; the launch traced here: 234 us
  waiting for transfers between devices  122 us (52%)
  blocking collectives  56.7 us (24%)
  other arithmetic  21.2 us (9%)
  between operations  16.5 us (7%)
  matrix products  11.9 us (5%)
  local copies, waits for them, and re-layouts  5.68 us (2%)
    all_gather x2, waiting for transfers between devices, window_of(): lax.all_gather(select(tiles_in, wanted), 'second')  96.8 us
    psum x1, blocking collectives, local(): lax.psum(jnp.sum((corrected - predicted) ** 2), ('past', 'second'))  39.5 us
    reduce_scatter x2, waiting for transfers between devices, shared(): lax.psum_scatter(memory(tiles_in), 'past', scatter_dimension=0, tiled=True)  25.3 us
    all_gather x2, blocking collectives, spread(): return lax.all_gather(piece, 'past', axis=0, tiled=True)  17.2 us
    dot_general x2, matrix products, memory(): jnp.einsum('cqpij,qpsjk->csik', left_side, right_side, precision=lax.Prec...  8.27 us
    reduce_sum x2, other arithmetic, window_of(): jnp.sum(lax.all_gather(select(tiles_in, wanted), 'second'), axis=0)  5.67 us
  transfers between devices with their start and end apart: 4, of which 4 were waited for; matrix products, arithmetic and copies ran while one was open for 4% of the time, Pallas kernels for 0%

profile of v1, /device:TPU:0, one launch (start us, length us, event | category | flops | bytes accessed | tf_op | source)
XLA Modules:
  0.0 234.3 jit_solution(4242096481114986341)
XLA Ops:
  7.2 0.0 all-gather.5.cloned.1.call-start
  7.9 1.6 gather_fusion.1
  9.5 0.8 select_select_fusion.1
  10.3 0.0 reduce-scatter.3.cloned.1.call-start
  10.4 0.7 compare_select_fusion.1
  11.1 0.6 gather_fusion
  11.7 0.7 and_select_fusion
  12.4 3.0 %fusion.2 = f32[4,16,64,64]{3,2,0,1:T(8,128)S(1)} fusion(f32[4,16,64,128]{3,2,1,0:T(8,128)} %param.9), kind=kLoop, calls=%fused_computation.7 | loop fusion | flops 786432 | bytes 5242880 | tf_op jit(solution)/shard_map/add | solution.py:16
  15.4 2.2 copy_bitcast_fusion
  17.5 46.3 %all-gather.5.cloned.1.call-done = f32[128,64,128]{2,1,0:T(8,128)} async-done(((f32[8,64,128]{2,1,0:T(8,128)}), f32[128,64,128]{2,1,0:T(8,128)}) %all-gather.5.cloned.1.call-update) | async-done | bytes 4194320 | tf_op jit(solution)/shard_map/all_gather | solution.py:44
  63.8 2.5 %reduce_sum.27 = f32[8,64,128]{2,1,0:T(8,128)S(1)} reduce(f32[16,8,64,128]{3,2,1,0:T(8,128)} %bitcast.107, f32[]{:T(128)} %constant.37.clone.1), dimensions={0}, to_apply=%region_0.0 | reduce | flops 983040 | bytes 4456452 | tf_op jit(solution)/shard_map/reduce_sum | solution.py:44
  66.3 0.1 fusion.31
  66.5 0.1 fusion.34
  66.6 0.1 maximum_bitcast_fusion.11
  66.7 4.1 %fusion.5 = f32[2,16,64,128]{3,2,1,0:T(8,128)S(1)} fusion(f32[1,4,16,64,128]{4,3,0,1,2:T(8,128)} %get-tuple-element.8, f32[1,4,16,64,128]{4,3,0,1,2:T(8,128)S(1)} %get-tuple-element.7, f32[1,2,4,64,64]{4,3,1,2,0:T(8,128)S(1)} %get-tuple-element.28, f32[1,2,4,64,64]{4,3,1,2,0:T(8,128)S(1)} %get-tuple-element.27), kind=kOutput, calls=%fused_computation.12 | convolution fusion | flops 1611726848 | bytes 5505024 | tf_op jit(solution)/shard_map/cqpij,qpsjk->csik/dot_general | solution.py:52
  70.9 0.2 slice_negate_fusion.1
  71.1 1.0 fusion.14
  72.2 0.0 all-gather.7.cloned.1.call-start
  72.2 0.1 fusion.65
  72.3 0.1 copy.49
  72.4 0.1 copy.32
  72.5 0.1 dynamic-slice_negate_fusion
  72.6 0.4 fusion.28
  73.0 12.5 %reduce-scatter.3.cloned.1.call-done = f32[8,64,128]{2,1,0:T(8,128)} async-done(((f32[16,64,128]{2,1,0:T(8,128)}), f32[8,64,128]{2,1,0:T(8,128)}) %reduce-scatter.3.cloned.1.call-update) | async-done | bytes 262160 | tf_op jit(solution)/shard_map/reduce_scatter | solution.py:70
  85.5 1.5 fusion.10
  87.0 0.1 fusion.64
  87.1 0.1 multiply_add_fusion
  87.2 8.7 %all_gather.20 = f32[16,64,128]{2,1,0:T(8,128)} all-gather(f32[8,64,128]{2,1,0:T(8,128)S(1)} %multiply_add_fusion), channel_id=1, replica_groups=mesh['past'=2,'second'=16] {'past'}, dimensions={0}, use_global_device_ids=true | all-gather | bytes 786432 | tf_op jit(solution)/shard_map/all_gather | solution.py:73
  95.9 2.3 gather_fusion.2
  98.2 1.7 select_select_fusion
  100.0 0.0 reduce-scatter.5.cloned.1.call-start
  100.0 50.5 %all-gather.7.cloned.1.call-done = f32[128,64,128]{2,1,0:T(8,128)} async-done(((f32[8,64,128]{2,1,0:T(8,128)}), f32[128,64,128]{2,1,0:T(8,128)}) %all-gather.7.cloned.1.call-update) | async-done | bytes 4194320 | tf_op jit(solution)/shard_map/all_gather | solution.py:44
  150.5 3.2 %reduce_sum.28 = f32[8,64,128]{2,1,0:T(8,128)} reduce(f32[16,8,64,128]{3,2,1,0:T(8,128)} %bitcast.108, f32[]{:T(128)} %constant.37.clone.1), dimensions={0}, to_apply=%region_2.4 | reduce | flops 983040 | bytes 4456452 | tf_op jit(solution)/shard_map/reduce_sum | solution.py:44
  153.7 1.1 fusion.30
  154.8 1.0 fusion.37
  155.8 0.1 maximum_bitcast_fusion.10
  156.0 4.1 %fusion.6 = f32[2,16,64,128]{3,2,1,0:T(8,128)S(1)} fusion(f32[1,4,16,64,128]{4,3,0,1,2:T(8,128)} %get-tuple-element.8, f32[1,4,16,64,128]{4,3,0,1,2:T(8,128)S(1)} %get-tuple-element.7, f32[1,2,4,64,64]{4,3,2,1,0:T(8,128)S(1)} %get-tuple-element.24, f32[1,2,4,64,64]{4,3,2,1,0:T(8,128)S(1)} %get-tuple-element.23), kind=kOutput, calls=%fused_computation.13 | convolution fusion | flops 1611726848 | bytes 5505024 | tf_op jit(solution)/shard_map/cqpij,qpsjk->csik/dot_general | solution.py:52
  160.1 0.2 slice_negate_fusion
  160.4 1.0 fusion.12
  161.4 0.4 fusion.41
  161.8 0.1 slice_negate_fusion.3
  161.9 12.8 %reduce-scatter.5.cloned.1.call-done = f32[8,64,128]{2,1,0:T(8,128)} async-done(((f32[16,64,128]{2,1,0:T(8,128)}), f32[8,64,128]{2,1,0:T(8,128)}) %reduce-scatter.5.cloned.1.call-update) | async-done | bytes 262160 | tf_op jit(solution)/shard_map/reduce_scatter | solution.py:70
  174.7 1.5 fusion.8
  176.2 0.1 fusion.63
  176.3 0.8 multiply_reduce_fusion
  177.1 8.5 %all_gather.23 = f32[16,64,128]{2,1,0:T(8,128)S(1)} all-gather(f32[8,64,128]{2,1,0:T(8,128)S(1)} %get-tuple-element.4), channel_id=1, replica_groups=mesh['past'=2,'second'=16] {'past'}, dimensions={0}, use_global_device_ids=true | all-gather | bytes 786432 | tf_op jit(solution)/shard_map/all_gather | solution.py:73
  185.7 39.5 %psum.7 = f32[]{:T(128)} all-reduce(f32[]{:T(128)} %get-tuple-element.3), channel_id=1, replica_groups=mesh['past'=2,'second'=16] {'past','second'}, use_global_device_ids=true, to_apply=%region_5.7 | all-reduce | flops 1 | bytes 8 | tf_op jit(solution)/shard_map/psum | solution.py:80
  225.8 0.8 copy.58
  (17 shorter events, 0.2 us)
Async XLA Ops:
  7.2 3.9 %copy-start = (f32[8]{0:T(128)S(1)}, f32[8]{0:T(128)}, u32[]{:S(2)}) copy-start(f32[8]{0:T(128)} %param.11) | copy-start | bytes 100
  7.2 56.7 %all-gather.5.cloned.1.call-start = ((), (), s32[]{:S(2)}) async-start(), calls=%async_computation.4 | async-start | bytes 4456448 | tf_op jit(solution)/shard_map/all_gather | solution.py:44
  10.3 75.1 %reduce-scatter.3.cloned.1.call-start = ((), (), s32[]{:S(2)}) async-start(), calls=%async_computation.2 | async-start | bytes 786432 | tf_op jit(solution)/shard_map/reduce_scatter | solution.py:70
  12.4 3.0 %copy-start.1 = (f32[4,16,64,128]{3,2,1,0:T(8,128)S(1)}, f32[4,16,64,128]{3,2,1,0:T(8,128)}, u32[]{:S(2)}) copy-start(f32[4,16,64,128]{3,2,1,0:T(8,128)} %param.9) | copy-start | bytes 6291460
  70.9 1.3 copy-start.3
  70.9 1.6 copy-start.2
  72.2 78.3 %all-gather.7.cloned.1.call-start = ((), (), s32[]{:S(2)}) async-start(), calls=%async_computation.5 | async-start | bytes 4456448 | tf_op jit(solution)/shard_map/all_gather | solution.py:44
  100.0 74.7 %reduce-scatter.5.cloned.1.call-start = ((), (), s32[]{:S(2)}) async-start(), calls=%async_computation.3 | async-start | bytes 786432 | tf_op jit(solution)/shard_map/reduce_scatter | solution.py:70
Sparse Core Ops, SparseCore 0:
  10.7 53.0 all-gather.4
  72.3 13.1 reduce-scatter.2
  100.1 50.3 all-gather.6
  161.5 13.1 reduce-scatter.4
